TPU v7x, 512 devices: a whole 4x4x16 slice. The times are simulated.
512 devices in a mesh: row: 32 (over z, core), col: 16 (over y, x).
Axes of the slice: x: 4, y: 4, z: 16, core: 2. Of those that a mesh axis runs over, the one named last changes fastest.
Arguments:
- train_points: float32 [64, 32768], P(None, ('row', 'col')), may hold values from -6 to 6
- cand_points: float32 [64, 32768], P(None, ('row', 'col')), may hold values from -6 to 6
- inv_length: float32 [64], replicated, may hold values from 0.04 to 0.7
- noise: float32 [32768], P(('row', 'col')), may hold values from 0.5 to 4
- targets: float32 [16, 32768], P(None, ('row', 'col')), may hold values from -15 to 15
Outputs:
- solution: float32 [16, 32768], P(None, ('row', 'col'))
- post_mean: float32 [16, 32768], P(None, ('row', 'col'))
All inputs are finite; a program needn't handle non-finite values.
Results may differ from a plain program's by a relative error of at most 0.0047.
Values may be sent and summed in bfloat16 or wider, within the bound.
No kernel may reach another device: no remote copies, remote signals or barrier semaphores. Data moves between devices by JAX's collectives and lax.ppermute only.
A program may use at most 64 MiB of HBM per device.

v0:
```python
import math
import jax
import jax.numpy as jnp
from jax import lax
from jax.sharding import PartitionSpec as P

ITERS = 2
root_five = math.sqrt(5.0)


def matern(left, left_norm, right, right_norm):
    inner = lax.dot_general(
        left, right, (((0,), (0,)), ((), ())), preferred_element_type=jnp.float32
    )
    dist_sq = jnp.maximum(left_norm[:, None] + right_norm[None, :] - 2.0 * inner, 0.0)
    radius = jnp.sqrt(dist_sq)
    return (1.0 + root_five * radius + 5.0 / 3.0 * dist_sq) * jnp.exp(-root_five * radius)


def tile_rows(amount):
    best = 1
    for candidate in range(1, 513):
        if amount % candidate == 0:
            best = candidate
    return best


def accumulate(carried, vector_piece, piece_points, piece_norms, other, other_norms):
    amount = vector_piece.shape[1]
    block = tile_rows(amount)

    def advance(block_index, running):
        offset = block_index * block
        sub_points = lax.dynamic_slice_in_dim(piece_points, offset, block, 1)
        sub_norms = lax.dynamic_slice_in_dim(piece_norms, offset, block, 0)
        sub_vector = lax.dynamic_slice_in_dim(vector_piece, offset, block, 1)
        kernel_tile = matern(sub_points, sub_norms, other, other_norms)
        return running + jnp.dot(
            sub_vector,
            kernel_tile,
            precision=lax.Precision.HIGHEST,
            preferred_element_type=jnp.float32,
        )

    return lax.fori_loop(0, amount // block, advance, carried)


def per_device(train_points, cand_points, inv_length, noise, targets):
    scaled_train = (train_points * inv_length[:, None]).astype(jnp.bfloat16)
    scaled_cand = (cand_points * inv_length[:, None]).astype(jnp.bfloat16)
    row_train, row_cand = (
        lax.all_gather(scaled_train, "col", axis=1, tiled=True),
        lax.all_gather(scaled_cand, "col", axis=1, tiled=True),
    )
    col_train = lax.all_gather(scaled_train, "row", axis=1, tiled=True)
    row_norms = jnp.sum(jnp.square(row_train.astype(jnp.float32)), axis=0)
    cand_norms = jnp.sum(jnp.square(row_cand.astype(jnp.float32)), axis=0)
    col_norms = jnp.sum(jnp.square(col_train.astype(jnp.float32)), axis=0)
    outputs = targets.shape[0]

    def from_columns(other, other_norms, carried, vector_piece):
        return accumulate(carried, vector_piece, col_train, col_norms, other, other_norms)

    def squares(residual):
        return lax.psum(jnp.sum(residual * residual, axis=1), ("row", "col"))

    solution = jnp.zeros_like(targets)
    residual = targets
    direction = targets
    norm_now = squares(residual)
    for iteration in range(ITERS):
        start_total = jnp.zeros((outputs, row_train.shape[1]), jnp.float32)
        partial_image = from_columns(
            row_train, row_norms, start_total, lax.all_gather(direction, "row", axis=1, tiled=True)
        )
        own_image = lax.psum_scatter(partial_image, "col", scatter_dimension=1, tiled=True)
        image = own_image + noise[None, :] * direction
        alpha = norm_now / lax.psum(jnp.sum(direction * image, axis=1), ("row", "col"))
        solution = solution + alpha[:, None] * direction
        residual = residual - alpha[:, None] * image
        norm_next = squares(residual)
        direction = residual + (norm_next / norm_now)[:, None] * direction
        norm_now = norm_next
    mean_start = jnp.zeros((outputs, row_cand.shape[1]), jnp.float32)
    partial_mean = from_columns(
        row_cand, cand_norms, mean_start, lax.all_gather(solution, "row", axis=1, tiled=True)
    )
    post_mean = lax.psum_scatter(partial_mean, "col", scatter_dimension=1, tiled=True)
    return (solution, post_mean)


def solution(mesh):
    placed = (
        P(None, ("row", "col")),
        P(None, ("row", "col")),
        P(),
        P(("row", "col")),
        P(None, ("row", "col")),
    )
    return jax.shard_map(
        per_device,
        mesh=mesh,
        in_specs=placed,
        out_specs=(P(None, ("row", "col")), P(None, ("row", "col"))),
        check_vma=False,
    )
```

profile of v0, /device:TPU:2, one launch (start us, length us, event | category | flops | bytes accessed | tf_op | source)
XLA Modules:
  0.0 763.7 jit_solution(8951887657408759057)
XLA Ops:
  9.6 37.6 %all_gather.19 = bf16[64,2048]{0,1:T(8,128)(2,1)S(1)} all-gather(bf16[64,64]{0,1:T(8,128)(2,1)S(1)} %get-tuple-element.538), channel_id=1, replica_groups=mesh['row'=32,'col'=16] {'row'}, dimensions={1}, use_global_device_ids=true | all-gather | bytes 270336 | tf_op jit(solution)/shard_map/all_gather | solution.py:55
  47.8 23.8 %all_gather.20 = bf16[64,1024]{0,1:T(8,128)(2,1)S(1)} all-gather(bf16[64,64]{0,1:T(8,128)(2,1)S(1)} %get-tuple-element.538), channel_id=1, replica_groups=mesh['row'=32,'col'=16] {'col'}, dimensions={1}, use_global_device_ids=true | all-gather | bytes 139264 | tf_op jit(solution)/shard_map/all_gather | solution.py:52
  71.9 27.5 %all-gather = f32[32,64,16]{1,2,0:T(8,128)S(1)} all-gather(f32[1,64,16]{1,2,0:T(8,128)S(1)} %bitcast.37), channel_id=1, replica_groups=mesh['row'=32,'col'=16] {'row'}, dimensions={0}, use_global_device_ids=true | all-gather | bytes 135168 | tf_op jit(solution)/shard_map/all_gather | solution.py:74
  99.6 11.9 %while.42 = (s32[]{:T(128)}, f32[16,1024]{1,0:T(8,128)S(1)}, f32[16,2048]{1,0:T(8,128)S(1)}, f32[2048]{0:T(1024)S(1)}, f32[1024]{0:T(1024)S(1)}, /*index=5*/bf16...) while((s32[]{:T(128)}, f32[16,1024]{1,0:T(8,128)S(1)}, ...), condition=%wide.region_5.0_spmd.clone, body=%wide.region_4.0_spmd.clone.sunk | while | flops 173047808 | bytes 4565169 | solution.py:45
  100.2 2.4 fusion.132
  103.2 2.4 fusion.132
  106.1 2.4 fusion.132
  109.1 2.4 fusion.132
  112.6 83.7 %reduce-scatter.10.cloned.1.call-done = f32[64,16]{1,0:T(8,128)} async-done(((f32[1024,16]{1,0:T(8,128)}), f32[64,16]{1,0:T(8,128)}) %reduce-scatter.10.cloned.1.call-update) | async-done | bytes 4112
  197.3 101.8 %all-reduce = (f32[16]{0:T(128)S(1)}, f32[16]{0:T(128)S(1)}) all-reduce(f32[16]{0:T(128)S(1)} %get-tuple-element.492, f32[16]{0:T(128)S(1)} %get-tuple-element.491), channel_id=1, replica_groups=mesh['row'=32,'col'=16] {'row','col'}, use_global_device_ids=true, to_apply=%region_1.0 | all-reduce | flops 32 | bytes 256 | tf_op jit(solution)/shard_map/psum | solution.py:65
  299.3 100.8 %psum.30 = f32[16]{0:T(128)S(1)} all-reduce(f32[16]{0:T(128)S(1)} %multiply_reduce_fusion.4), channel_id=1, replica_groups=mesh['row'=32,'col'=16] {'row','col'}, use_global_device_ids=true, to_apply=%region_10.0 | all-reduce | flops 16 | bytes 128 | tf_op jit(solution)/shard_map/psum | solution.py:65
  400.3 28.5 %all-gather.1 = f32[32,64,16]{1,2,0:T(8,128)S(1)} all-gather(f32[1,64,16]{1,2,0:T(8,128)S(1)} %fusion.105), channel_id=1, replica_groups=mesh['row'=32,'col'=16] {'row'}, dimensions={0}, use_global_device_ids=true | all-gather | bytes 135168 | tf_op jit(solution)/shard_map/all_gather | solution.py:74
  429.0 11.9 %while.43 = (s32[]{:T(128)}, f32[16,1024]{1,0:T(8,128)S(1)}, f32[16,2048]{1,0:T(8,128)S(1)}, f32[2048]{0:T(1024)S(1)}, f32[1024]{0:T(1024)S(1)}, /*index=5*/bf16...) while((s32[]{:T(128)}, f32[16,1024]{1,0:T(8,128)S(1)}, ...), condition=%wide.region_12.0_spmd.clone, body=%wide.region_11.0_spmd.clone.sunk | while | flops 173047808 | bytes 4565169 | solution.py:45
  429.5 2.4 fusion.138
  432.5 2.4 fusion.138
  435.5 2.4 fusion.138
  438.5 2.4 fusion.138
  442.0 22.1 %all_gather.23 = bf16[64,1024]{0,1:T(8,128)(2,1)S(1)} all-gather(bf16[64,64]{0,1:T(8,128)(2,1)S(1)} %get-tuple-element.537), channel_id=1, replica_groups=mesh['row'=32,'col'=16] {'col'}, dimensions={1}, use_global_device_ids=true | all-gather | bytes 139264 | tf_op jit(solution)/shard_map/all_gather | solution.py:53
  464.4 60.8 %reduce-scatter.12.cloned.1.call-done = f32[64,16]{1,0:T(8,128)} async-done(((f32[1024,16]{1,0:T(8,128)}), f32[64,16]{1,0:T(8,128)}) %reduce-scatter.12.cloned.1.call-update) | async-done | bytes 4112
  526.2 102.1 %psum.31 = f32[16]{0:T(128)S(1)} all-reduce(f32[16]{0:T(128)S(1)} %multiply_reduce_fusion.3), channel_id=1, replica_groups=mesh['row'=32,'col'=16] {'row','col'}, use_global_device_ids=true, to_apply=%region_15.0 | all-reduce | flops 16 | bytes 128 | tf_op jit(solution)/shard_map/psum | solution.py:78
  628.4 28.8 %all-gather.2 = f32[32,64,16]{1,2,0:T(8,128)S(1)} all-gather(f32[1,64,16]{1,2,0:T(8,128)S(1)} %bitcast.44), channel_id=1, replica_groups=mesh['row'=32,'col'=16] {'row'}, dimensions={0}, use_global_device_ids=true | all-gather | bytes 135168 | tf_op jit(solution)/shard_map/all_gather | solution.py:86
  657.4 11.9 %while.44 = (s32[]{:T(128)}, f32[16,1024]{1,0:T(8,128)S(1)}, f32[16,2048]{1,0:T(8,128)S(1)}, f32[2048]{0:T(1024)S(1)}, f32[1024]{0:T(1024)S(1)}, /*index=5*/bf16...) while((s32[]{:T(128)}, f32[16,1024]{1,0:T(8,128)S(1)}, ...), condition=%wide.region_18.0_spmd.clone, body=%wide.region_17.0_spmd.clone.sunk | while | flops 173047808 | bytes 4565169 | solution.py:45
  658.0 2.4 fusion.144
  670.3 85.4 %reduce-scatter.14.cloned.1.call-done = f32[64,16]{1,0:T(8,128)} async-done(((f32[1024,16]{1,0:T(8,128)}), f32[64,16]{1,0:T(8,128)}) %reduce-scatter.14.cloned.1.call-update) | async-done | bytes 4112
  (71 shorter events, 24.9 us)
Async XLA Ops:
  7.2 64.7 %copy-start = (f32[16,64]{1,0:T(8,128)S(1)}, f32[16,64]{1,0:T(8,128)}, u32[]{:S(2)}) copy-start(f32[16,64]{1,0:T(8,128)} %param.15) | copy-start | bytes 12292
  7.2 189.2 %reduce-scatter.10.cloned.1.call-start = ((), (), s32[]{:S(2)}) async-start(), calls=%async_computation.3 | async-start | bytes 557056
  99.6 97.6 %copy-start.2 = (f32[64]{0:T(128)S(1)}, f32[64]{0:T(128)}, u32[]{:S(2)}) copy-start(f32[64]{0:T(128)} %param.14) | copy-start | bytes 772
  112.6 412.6 %reduce-scatter.12.cloned.1.call-start = ((), (), s32[]{:S(2)}) async-start(), calls=%async_computation.4 | async-start | bytes 557056
  441.9 313.8 %reduce-scatter.14.cloned.1.call-start = ((), (), s32[]{:S(2)}) async-start(), calls=%async_computation.5 | async-start | bytes 557056
  628.4 29.0 %copy-start.1 = (f32[16,64]{1,0:T(8,128)}, f32[16,64]{1,0:T(8,128)S(1)}, u32[]{:S(2)}) copy-start(f32[16,64]{1,0:T(8,128)S(1)} %multiply_add_fusion) | copy-start | bytes 12292
Sparse Core Ops, SparseCore 0:
  112.7 83.6 reduce-scatter.9
  442.1 83.1 reduce-scatter.11
  670.5 85.2 reduce-scatter.13
where the time goes:
time: 764 us
  blocking collectives  473 us (62%)
  waiting for transfers between devices  230 us (30%)
  matrix products  34.7 us (5%)
  between operations  13.9 us (2%)
  local copies, waits for them, and re-layouts  9.77 us (1%)
    unnamed x6, waiting for transfers between devices  230 us
    psum x2, blocking collectives, squares(): return lax.psum(jnp.sum(residual * residual, axis=1), ('row', 'col'))  203 us
    psum x1, blocking collectives, per_device(): lax.psum(jnp.sum(direction * image, axis=1), ('row', 'col'))  102 us
    all_gather x2, blocking collectives, per_device(): lax.all_gather(direction, 'row', axis=1, tiled=True)  56 us
    all_gather x1, blocking collectives, per_device(): col_train = lax.all_gather(scaled_train, 'row', axis=1, tiled=True)  37.6 us
    dot_general x12, matrix products, advance(): jnp.dot(sub_vector, kernel_tile, precision=lax.Precision.HIGHEST, preferr...  29.1 us
    all_gather x1, blocking collectives, per_device(): lax.all_gather(solution, 'row', axis=1, tiled=True)  28.8 us
    all_gather x1, blocking collectives, per_device(): lax.all_gather(scaled_train, 'col', axis=1, tiled=True)  23.8 us
  transfers between devices with their start and end apart: 3, of which 3 were waited for; matrix products, arithmetic and copies ran while one was open for 0% of the time, Pallas kernels for 0%

commit v1 on v0

--- a/solution.py
+++ b/solution.py
@@ -62,7 +62,7 @@
         return accumulate(carried, vector_piece, col_train, col_norms, other, other_norms)
 
     def squares(residual):
-        return lax.psum(jnp.sum(residual * residual, axis=1), ("row", "col"))
+        return lax.psum(lax.psum(jnp.sum(residual * residual, axis=1), "col"), "row")
 
     solution = jnp.zeros_like(targets)
     residual = targets

time: 764 us -> 829 us (1.085)
  blocking collectives: 473 us -> 536 us
    psum x1 -> x2, blocking collectives: 102 us -> 203 us  [per_device(): lax.psum(jnp.sum(direction * image, axis=1), ('row', 'col'))]
    psum x2 -> x4, blocking collectives: 203 us -> 166 us  [the longest x2 92.2 us: squares(): lax.psum(lax.psum(jnp.sum(residual * residual, axis=1), 'col'), 'row')]
where the time goes in v1:
time: 829 us; the launch traced here: 828 us
  blocking collectives  536 us (65%)
  waiting for transfers between devices  231 us (28%)
  matrix products  34.7 us (4%)
  between operations  13.9 us (2%)
  local copies, waits for them, and re-layouts  9.76 us (1%)
    unnamed x6, waiting for transfers between devices  231 us
    psum x2, blocking collectives, per_device(): lax.psum(jnp.sum(direction * image, axis=1), ('row', 'col'))  203 us
    psum x2, blocking collectives, squares(): lax.psum(lax.psum(jnp.sum(residual * residual, axis=1), 'col'), 'row')  92.2 us
    psum x2, blocking collectives, squares(): lax.psum(jnp.sum(residual * residual, axis=1), 'col')  73.8 us
    all_gather x2, blocking collectives, per_device(): lax.all_gather(direction, 'row', axis=1, tiled=True)  55.2 us
    all_gather x1, blocking collectives, per_device(): col_train = lax.all_gather(scaled_train, 'row', axis=1, tiled=True)  37.6 us
    dot_general x12, matrix products, advance(): jnp.dot(sub_vector, kernel_tile, precision=lax.Precision.HIGHEST, preferr...  29.1 us
    all_gather x1, blocking collectives, per_device(): lax.all_gather(solution, 'row', axis=1, tiled=True)  29 us
  transfers between devices with their start and end apart: 3, of which 3 were waited for; matrix products, arithmetic and copies ran while one was open for 0% of the time, Pallas kernels for 0%

profile of v1, /device:TPU:2, one launch (start us, length us, event | category | flops | bytes accessed | tf_op | source)
XLA Modules:
  0.0 828.1 jit_solution(1754194843599600129)
XLA Ops:
  9.6 37.6 %all_gather.19 = bf16[64,2048]{0,1:T(8,128)(2,1)S(1)} all-gather(bf16[64,64]{0,1:T(8,128)(2,1)S(1)} %get-tuple-element.536), channel_id=1, replica_groups=mesh['row'=32,'col'=16] {'row'}, dimensions={1}, use_global_device_ids=true | all-gather | bytes 270336 | tf_op jit(solution)/shard_map/all_gather | solution.py:55
  47.8 23.8 %all_gather.20 = bf16[64,1024]{0,1:T(8,128)(2,1)S(1)} all-gather(bf16[64,64]{0,1:T(8,128)(2,1)S(1)} %get-tuple-element.536), channel_id=1, replica_groups=mesh['row'=32,'col'=16] {'col'}, dimensions={1}, use_global_device_ids=true | all-gather | bytes 139264 | tf_op jit(solution)/shard_map/all_gather | solution.py:52
  71.9 27.5 %all-gather = f32[32,64,16]{1,2,0:T(8,128)S(1)} all-gather(f32[1,64,16]{1,2,0:T(8,128)S(1)} %bitcast.37), channel_id=1, replica_groups=mesh['row'=32,'col'=16] {'row'}, dimensions={0}, use_global_device_ids=true | all-gather | bytes 135168 | tf_op jit(solution)/shard_map/all_gather | solution.py:74
  99.6 11.9 %while.42 = (s32[]{:T(128)}, f32[16,1024]{1,0:T(8,128)S(1)}, f32[16,2048]{1,0:T(8,128)S(1)}, f32[2048]{0:T(1024)S(1)}, f32[1024]{0:T(1024)S(1)}, /*index=5*/bf16...) while((s32[]{:T(128)}, f32[16,1024]{1,0:T(8,128)S(1)}, ...), condition=%wide.region_6.0_spmd.clone, body=%wide.region_5.0_spmd.clone.sunk | while | flops 173047808 | bytes 4565169 | solution.py:45
  100.2 2.4 fusion.132
  103.2 2.4 fusion.132
  106.1 2.4 fusion.132
  109.1 2.4 fusion.132
  112.6 83.7 %reduce-scatter.10.cloned.1.call-done = f32[64,16]{1,0:T(8,128)} async-done(((f32[1024,16]{1,0:T(8,128)}), f32[64,16]{1,0:T(8,128)}) %reduce-scatter.10.cloned.1.call-update) | async-done | bytes 4112
  197.3 36.3 %psum.42 = f32[16]{0:T(128)S(1)} all-reduce(f32[16]{0:T(128)S(1)} %get-tuple-element.492), channel_id=1, replica_groups=mesh['row'=32,'col'=16] {'col'}, use_global_device_ids=true, to_apply=%region_1.0 | all-reduce | flops 16 | bytes 128 | tf_op jit(solution)/shard_map/psum | solution.py:65
  233.6 46.5 %psum.43 = f32[16]{0:T(128)S(1)} all-reduce(f32[16]{0:T(128)S(1)} %psum.42), channel_id=1, replica_groups=mesh['row'=32,'col'=16] {'row'}, use_global_device_ids=true, to_apply=%region_2.0 | all-reduce | flops 16 | bytes 128 | tf_op jit(solution)/shard_map/psum | solution.py:65
  280.1 100.7 %psum.44 = f32[16]{0:T(128)S(1)} all-reduce(f32[16]{0:T(128)S(1)} %get-tuple-element.491), channel_id=1, replica_groups=mesh['row'=32,'col'=16] {'row','col'}, use_global_device_ids=true, to_apply=%region_9.0 | all-reduce | flops 16 | bytes 128 | tf_op jit(solution)/shard_map/psum | solution.py:78
  381.0 37.5 %psum.45 = f32[16]{0:T(128)S(1)} all-reduce(f32[16]{0:T(128)S(1)} %multiply_reduce_fusion.4), channel_id=1, replica_groups=mesh['row'=32,'col'=16] {'col'}, use_global_device_ids=true, to_apply=%region_11.0 | all-reduce | flops 16 | bytes 128 | tf_op jit(solution)/shard_map/psum | solution.py:65
  418.4 45.8 %psum.46 = f32[16]{0:T(128)S(1)} all-reduce(f32[16]{0:T(128)S(1)} %psum.45), channel_id=1, replica_groups=mesh['row'=32,'col'=16] {'row'}, use_global_device_ids=true, to_apply=%region_12.0 | all-reduce | flops 16 | bytes 128 | tf_op jit(solution)/shard_map/psum | solution.py:65
  464.3 27.7 %all-gather.1 = f32[32,64,16]{1,2,0:T(8,128)S(1)} all-gather(f32[1,64,16]{1,2,0:T(8,128)S(1)} %fusion.105), channel_id=1, replica_groups=mesh['row'=32,'col'=16] {'row'}, dimensions={0}, use_global_device_ids=true | all-gather | bytes 135168 | tf_op jit(solution)/shard_map/all_gather | solution.py:74
  492.2 11.9 %while.43 = (s32[]{:T(128)}, f32[16,1024]{1,0:T(8,128)S(1)}, f32[16,2048]{1,0:T(8,128)S(1)}, f32[2048]{0:T(1024)S(1)}, f32[1024]{0:T(1024)S(1)}, /*index=5*/bf16...) while((s32[]{:T(128)}, f32[16,1024]{1,0:T(8,128)S(1)}, ...), condition=%wide.region_14.0_spmd.clone, body=%wide.region_13.0_spmd.clone.sunk | while | flops 173047808 | bytes 4565169 | solution.py:45
  492.7 2.4 fusion.138
  495.7 2.4 fusion.138
  505.2 22.2 %all_gather.23 = bf16[64,1024]{0,1:T(8,128)(2,1)S(1)} all-gather(bf16[64,64]{0,1:T(8,128)(2,1)S(1)} %get-tuple-element.535), channel_id=1, replica_groups=mesh['row'=32,'col'=16] {'col'}, dimensions={1}, use_global_device_ids=true | all-gather | bytes 139264 | tf_op jit(solution)/shard_map/all_gather | solution.py:53
  527.7 61.8 %reduce-scatter.12.cloned.1.call-done = f32[64,16]{1,0:T(8,128)} async-done(((f32[1024,16]{1,0:T(8,128)}), f32[64,16]{1,0:T(8,128)}) %reduce-scatter.12.cloned.1.call-update) | async-done | bytes 4112
  590.6 101.9 %psum.47 = f32[16]{0:T(128)S(1)} all-reduce(f32[16]{0:T(128)S(1)} %multiply_reduce_fusion.3), channel_id=1, replica_groups=mesh['row'=32,'col'=16] {'row','col'}, use_global_device_ids=true, to_apply=%region_17.0 | all-reduce | flops 16 | bytes 128 | tf_op jit(solution)/shard_map/psum | solution.py:78
  692.5 29.0 %all-gather.2 = f32[32,64,16]{1,2,0:T(8,128)S(1)} all-gather(f32[1,64,16]{1,2,0:T(8,128)S(1)} %bitcast.44), channel_id=1, replica_groups=mesh['row'=32,'col'=16] {'row'}, dimensions={0}, use_global_device_ids=true | all-gather | bytes 135168 | tf_op jit(solution)/shard_map/all_gather | solution.py:86
  721.7 11.9 %while.44 = (s32[]{:T(128)}, f32[16,1024]{1,0:T(8,128)S(1)}, f32[16,2048]{1,0:T(8,128)S(1)}, f32[2048]{0:T(1024)S(1)}, f32[1024]{0:T(1024)S(1)}, /*index=5*/bf16...) while((s32[]{:T(128)}, f32[16,1024]{1,0:T(8,128)S(1)}, ...), condition=%wide.region_20.0_spmd.clone, body=%wide.region_19.0_spmd.clone.sunk | while | flops 173047808 | bytes 4565169 | solution.py:45
  734.7 85.5 %reduce-scatter.14.cloned.1.call-done = f32[64,16]{1,0:T(8,128)} async-done(((f32[1024,16]{1,0:T(8,128)}), f32[64,16]{1,0:T(8,128)}) %reduce-scatter.14.cloned.1.call-update) | async-done | bytes 4112
  (74 shorter events, 32.2 us)
Async XLA Ops:
  7.2 64.7 %copy-start = (f32[16,64]{1,0:T(8,128)S(1)}, f32[16,64]{1,0:T(8,128)}, u32[]{:S(2)}) copy-start(f32[16,64]{1,0:T(8,128)} %param.15) | copy-start | bytes 12292
  7.2 189.2 %reduce-scatter.10.cloned.1.call-start = ((), (), s32[]{:S(2)}) async-start(), calls=%async_computation.3 | async-start | bytes 557056
  99.6 97.6 %copy-start.2 = (f32[64]{0:T(128)S(1)}, f32[64]{0:T(128)}, u32[]{:S(2)}) copy-start(f32[64]{0:T(128)} %param.14) | copy-start | bytes 772
  112.6 477.0 %reduce-scatter.12.cloned.1.call-start = ((), (), s32[]{:S(2)}) async-start(), calls=%async_computation.4 | async-start | bytes 557056
  505.1 315.0 %reduce-scatter.14.cloned.1.call-start = ((), (), s32[]{:S(2)}) async-start(), calls=%async_computation.5 | async-start | bytes 557056
  692.5 29.2 %copy-start.1 = (f32[16,64]{1,0:T(8,128)}, f32[16,64]{1,0:T(8,128)S(1)}, u32[]{:S(2)}) copy-start(f32[16,64]{1,0:T(8,128)S(1)} %multiply_add_fusion) | copy-start | bytes 12292
Sparse Core Ops, SparseCore 0:
  112.7 83.6 reduce-scatter.9
  505.2 84.2 reduce-scatter.11
  734.8 85.3 reduce-scatter.13
